TPU v7x, 32 devices: a whole 2x2x4 slice. The times are simulated.
32 devices in a mesh: grp: 2 (over y), seq: 16 (over z, x, core).
Axes of the slice: x: 2, y: 2, z: 4, core: 2. Of those that a mesh axis runs over, the one named last changes fastest.
Arguments:
- queries: bfloat16 [4096, 128], P(('grp', 'seq')), parts along dimension 0, may hold values from -6 to 6
- keys: bfloat16 [4096, 128], P(('grp', 'seq')), parts along dimension 0, may hold values from -6 to 6
- values: bfloat16 [4096, 128], P(('grp', 'seq')), parts along dimension 0, may hold values from -6 to 6
- log_gate: float32 [4096], P(('grp', 'seq')), parts along dimension 0, may hold values from -1 to 0, as said below
- out_grad: bfloat16 [4096, 128], P(('grp', 'seq')), parts along dimension 0, may hold values from -6 to 6
- segment_order: int32 [64], P(('grp', 'seq')), parts along dimension 0, may hold values from 0 to 31, each once
Outputs:
- attn_out: bfloat16 [4096, 128], P(('grp', 'seq')), parts along dimension 0
- query_grad: float32 [4096, 128], P(('grp', 'seq')), parts along dimension 0
- key_grad: float32 [4096, 128], P(('grp', 'seq')), parts along dimension 0
- value_grad: float32 [4096, 128], P(('grp', 'seq')), parts along dimension 0
- gate_grad: float32 [4096], P(('grp', 'seq')), parts along dimension 0
There are 2 independent parts, one for each index of `grp`. A program takes and returns all parts, laid end to end along the dimension named above; each array names one. Nothing has to cross between parts.
Inputs may be any that keep to these rules, and one draw needn't show every extreme that they name: `log_gate`: every gate is below one. `segment_order`: each segment index appears once.
All inputs are finite; a program needn't handle non-finite values.
Results may differ from a plain program's by a relative error of at most 0.0095.
Values may be sent and summed in bfloat16 or wider, within the bound.
No kernel may reach another device: no remote copies, remote signals or barrier semaphores. Data moves between devices by JAX's collectives and lax.ppermute only.
A program may use at most 64 MiB of HBM per device.

v0:
```python
import functools

import jax
import jax.numpy as jnp
from jax import lax
from jax.experimental import pallas as pl
from jax.experimental.pallas import tpu as pltpu
from jax.sharding import PartitionSpec as P


masked_value = -1e30


def contract_last(left, right):
    return lax.dot_general(
        left, right, (((1,), (1,)), ((), ())), preferred_element_type=jnp.float32
    )


def contract_first(left, right):
    return lax.dot_general(
        left, right, (((0,), (0,)), ((), ())), preferred_element_type=jnp.float32
    )


def tile_scores(query_rows, query_gate, query_pos, key_rows, key_gate, key_pos, score_scale):
    scores = (
        contract_last(query_rows, key_rows) * score_scale + query_gate[:, None] - key_gate[None, :]
    )
    visible = key_pos[None, :] <= query_pos[:, None]
    return (scores, visible)


def tile_probs(scores, visible, row_total):
    return jnp.where(visible, jnp.exp(scores - row_total[:, None]), 0.0)


def local_general(queries, keys, values, log_gate, out_grad, segment_order):
    tokens_here, width = queries.shape
    devices = lax.axis_size("seq")
    segment_rows = tokens_here // 2
    total_len = tokens_here * devices
    score_scale = width ** (-0.5)
    offsets_in = lax.broadcasted_iota(jnp.int32, (1, segment_rows), 1)
    local_cum = jnp.cumsum(log_gate.reshape(2, segment_rows), axis=1)
    segment_total = local_cum[:, -1]
    segment_place = segment_order.astype(jnp.float32)
    own_pos = (segment_order[:, None] * segment_rows + offsets_in).reshape(-1)
    all_totals, all_place = (
        lax.all_gather(segment_total, "seq", axis=0, tiled=True),
        lax.all_gather(segment_place, "seq", axis=0, tiled=True),
    )
    earlier = (all_place[None, :] < segment_place[:, None]).astype(jnp.float32)
    own_offset = jnp.sum(earlier * all_totals[None, :], axis=1)
    own_gate = (local_cum + own_offset[:, None]).reshape(-1)
    all_gate = lax.all_gather(own_gate, "seq", axis=0, tiled=True)
    all_pos = (all_place.astype(jnp.int32)[:, None] * segment_rows + offsets_in).reshape(-1)
    key_all, value_all = (
        lax.all_gather(keys, "seq", axis=0, tiled=True),
        lax.all_gather(values, "seq", axis=0, tiled=True),
    )
    block = 2048
    count = total_len // block

    def key_tile(block_index):
        start = block_index * block
        return (
            lax.dynamic_slice_in_dim(key_all, start, block),
            lax.dynamic_slice_in_dim(value_all, start, block),
            lax.dynamic_slice_in_dim(all_gate, start, block),
            lax.dynamic_slice_in_dim(all_pos, start, block),
        )

    def stats_step(block_index, carry):
        run_max, run_sum = carry
        key_rows, _, key_gate, key_pos = key_tile(block_index)
        scores, visible = tile_scores(
            queries, own_gate, own_pos, key_rows, key_gate, key_pos, score_scale
        )
        kept = jnp.where(visible, scores, masked_value)
        new_max = jnp.maximum(run_max, jnp.max(kept, axis=1))
        fresh = jnp.sum(jnp.where(visible, jnp.exp(kept - new_max[:, None]), 0.0), axis=1)
        return (new_max, run_sum * jnp.exp(run_max - new_max) + fresh)

    start_max = jnp.full((tokens_here,), masked_value, jnp.float32)
    run_max, run_sum = lax.fori_loop(
        0, count, stats_step, (start_max, jnp.zeros((tokens_here,), jnp.float32))
    )
    log_total = run_max + jnp.log(run_sum)

    def output_step(block_index, total):
        key_rows, value_rows, key_gate, key_pos = key_tile(block_index)
        scores, visible = tile_scores(
            queries, own_gate, own_pos, key_rows, key_gate, key_pos, score_scale
        )
        probs = tile_probs(scores, visible, log_total).astype(jnp.bfloat16)
        return total + jnp.dot(probs, value_rows, preferred_element_type=jnp.float32)

    out_full = lax.fori_loop(0, count, output_step, jnp.zeros((tokens_here, width), jnp.float32))
    attn_out = out_full.astype(jnp.bfloat16)
    row_delta = jnp.sum(out_grad.astype(jnp.float32) * out_full, axis=1)

    def row_terms(block_index):
        key_rows, value_rows, key_gate, key_pos = key_tile(block_index)
        scores, visible = tile_scores(
            queries, own_gate, own_pos, key_rows, key_gate, key_pos, score_scale
        )
        probs = tile_probs(scores, visible, log_total)
        dprob = contract_last(out_grad, value_rows)
        return (key_rows, probs, probs * (dprob - row_delta[:, None]))

    def query_step(block_index, total):
        key_rows, _, dscore = row_terms(block_index)
        return total + jnp.dot(
            dscore.astype(jnp.bfloat16), key_rows, preferred_element_type=jnp.float32
        )

    query_acc = lax.fori_loop(0, count, query_step, jnp.zeros((tokens_here, width), jnp.float32))
    query_all, grad_all = (
        lax.all_gather(queries, "seq", axis=0, tiled=True),
        lax.all_gather(out_grad, "seq", axis=0, tiled=True),
    )
    total_all, delta_all = (
        lax.all_gather(log_total, "seq", axis=0, tiled=True),
        lax.all_gather(row_delta, "seq", axis=0, tiled=True),
    )

    def column_step(block_index, carry):
        key_acc, value_acc, column_acc = carry
        start = block_index * block
        query_rows = lax.dynamic_slice_in_dim(query_all, start, block)
        grad_rows = lax.dynamic_slice_in_dim(grad_all, start, block)
        scores, visible = tile_scores(
            query_rows,
            lax.dynamic_slice_in_dim(all_gate, start, block),
            lax.dynamic_slice_in_dim(all_pos, start, block),
            keys,
            own_gate,
            own_pos,
            score_scale,
        )
        probs = tile_probs(scores, visible, lax.dynamic_slice_in_dim(total_all, start, block))
        dprob = contract_last(grad_rows, values)
        dscore = probs * (dprob - lax.dynamic_slice_in_dim(delta_all, start, block)[:, None])
        dscore_low = dscore.astype(jnp.bfloat16)
        key_acc = key_acc + contract_first(dscore_low, query_rows) * score_scale
        value_acc = value_acc + contract_first(probs.astype(jnp.bfloat16), grad_rows)
        column_acc = column_acc - jnp.sum(dscore, axis=0)
        return (key_acc, value_acc, column_acc)

    zeros_own = jnp.zeros((tokens_here, width), jnp.float32)
    key_grad, value_grad, gate_point = lax.fori_loop(
        0, count, column_step, (zeros_own, zeros_own, jnp.zeros((tokens_here,), jnp.float32))
    )
    query_grad = query_acc * score_scale
    point_rows = gate_point.reshape(2, segment_rows)
    within = jnp.flip(jnp.cumsum(jnp.flip(point_rows, 1), axis=1), 1)
    all_point = lax.all_gather(within[:, 0], "seq", axis=0, tiled=True)
    later = (all_place[None, :] > segment_place[:, None]).astype(jnp.float32)
    gate_grad = (within + jnp.sum(later * all_point[None, :], axis=1)[:, None]).reshape(-1)
    return (attn_out, query_grad, key_grad, value_grad, gate_grad)


LOG2E = 1.4426950408889634
META = 16


def pack_kernel(q_ref, k_ref, v_ref, g_ref, gate_hbm, order_hbm, out_ref, gate_ref, order_ref, sems):
    tokens = q_ref.shape[0]
    copies = [
        pltpu.make_async_copy(gate_hbm, gate_ref, sems.at[0]),
        pltpu.make_async_copy(order_hbm, order_ref, sems.at[1]),
    ]
    for index, ref in enumerate((q_ref, k_ref, v_ref, g_ref)):
        copies.append(
            pltpu.make_async_copy(
                ref, out_ref.at[pl.ds(index * tokens, tokens), :], sems.at[index + 2]
            )
        )
    for copy in copies:
        copy.start()
    copies[0].wait()
    copies[1].wait()
    gate = gate_ref[...]
    high = gate.astype(jnp.bfloat16).astype(jnp.float32)
    rest = gate - high
    mid = rest.astype(jnp.bfloat16).astype(jnp.float32)
    low = rest - mid
    lane = lax.broadcasted_iota(jnp.int32, (META, tokens), 1)
    row = lax.broadcasted_iota(jnp.int32, (META, tokens), 0)
    order = order_ref[...].astype(jnp.float32)
    place = jnp.where(lane < tokens // 2, order[:, 0:1], order[:, 1:2])
    meta = jnp.where(
        row == 0, high, jnp.where(row == 1, mid, jnp.where(row == 2, low, place))
    )
    out_ref[4 * tokens : 4 * tokens + META] = meta.astype(jnp.bfloat16)
    for copy in copies[2:]:
        copy.wait()


def split(items, turn, turns):
    return items[len(items) * turn // turns : len(items) * (turn + 1) // turns]


def block_order(steps):
    return list(range(steps))[::-1]


def sum_lanes(x, reverse):
    rows, lanes = x.shape
    pieces = []
    for _ in range(3):
        piece = x.astype(jnp.bfloat16)
        pieces.append(piece)
        x = x - piece.astype(jnp.float32)
    source = lax.broadcasted_iota(jnp.int32, (lanes, lanes), 0)
    target = lax.broadcasted_iota(jnp.int32, (lanes, lanes), 1)
    ones = (source >= target if reverse else source <= target).astype(jnp.float32)
    sums = jnp.dot(
        jnp.concatenate(pieces, axis=0),
        ones.astype(jnp.bfloat16),
        preferred_element_type=jnp.float32,
    )
    return (sums[2 * rows :] + sums[rows : 2 * rows]) + sums[:rows]


def roll_sum_rows(x, reverse):
    rows = x.shape[0]
    row = lax.broadcasted_iota(jnp.int32, x.shape, 0)
    step = 1
    while step < rows:
        if reverse:
            x = x + jnp.where(row < rows - step, pltpu.roll(x, rows - step, 0), 0.0)
        else:
            x = x + jnp.where(row >= step, pltpu.roll(x, step, 0), 0.0)
        step *= 2
    return x


def spread(column, width):
    return jnp.broadcast_to(column, (column.shape[0], width))


def halves(x, width):
    return [x[:, at : at + width] for at in range(0, x.shape[1], width)]


def log_total_of(pieces, width):
    best = pieces[0]
    for s in pieces[1:]:
        best = jnp.maximum(best, s)
    top = spread(jnp.max(best, axis=1, keepdims=True), width)
    mass = jnp.exp2(pieces[0] - top)
    for s in pieces[1:]:
        mass = mass + jnp.exp2(s - top)
    return top + spread(jnp.log2(jnp.sum(mass, axis=1, keepdims=True)), width)


def score_of(q, ks, key_row, tile, cols, factor):
    c0 = tile * cols
    return contract_last(q, ks[c0 : c0 + cols, :]) * factor - key_row[:, c0 : c0 + cols]


def start_rows(own, place, ks, key_row, own_s, own_total):
    total, width = ks.shape
    tokens = own_s.shape[0]
    seg = tokens // 2
    cols = 2 * tokens
    inner = lax.broadcasted_iota(jnp.int32, (tokens, 1), 0)
    row_pos = jnp.where(inner < seg, place[0] * seg + inner, place[1] * seg + inner - seg)
    q = own[0:tokens, :]
    pieces = []
    for tile in range(total // cols):
        c0 = tile * cols
        seen = lax.broadcasted_iota(jnp.int32, (tokens, cols), 1) + c0 <= row_pos
        s = score_of(q, ks, key_row, tile, cols, width ** (-0.5) * LOG2E)
        s = jnp.where(seen, s, masked_value)
        own_s[:, c0 : c0 + cols] = s
        pieces += halves(s, width)
    own_total[...] = log_total_of(pieces, width)


def row_kernel(own, ks, vs, own_s, own_total, out_ref, dq_ref):
    total, width = ks.shape
    tokens = out_ref.shape[0]
    cols = 2 * tokens
    g = own[3 * tokens : 4 * tokens, :]
    log_total = own_total[...]
    p, dps = [], []
    for tile in range(total // cols):
        c0 = tile * cols
        p += [jnp.exp2(s - log_total) for s in halves(own_s[:, c0 : c0 + cols], width)]
        dps += halves(contract_last(g, vs[c0 : c0 + cols, :]), width)
    low = jnp.concatenate([t.astype(jnp.bfloat16) for t in p], axis=1)
    out = jnp.dot(low, vs[...], preferred_element_type=jnp.float32)
    out_ref[...] = out.astype(jnp.bfloat16)
    delta = spread(jnp.sum(g.astype(jnp.float32) * out, axis=1, keepdims=True), width)
    low = jnp.concatenate(
        [(t * (dp - delta)).astype(jnp.bfloat16) for t, dp in zip(p, dps)], axis=1
    )
    dq_ref[...] = width ** (-0.5) * jnp.dot(low, ks[...], preferred_element_type=jnp.float32)


def core_kernel(counts, partner, tokens, width, core_ref, *refs):
    blocks = refs[: len(counts)]
    keep_ref, send_ref, ks, vs, own_s, own_total = refs[len(counts) : len(counts) + 6]
    qs, gs, cums, key_row, points, lines = refs[len(counts) + 6 :]
    seg = tokens // 2
    total = qs.shape[0]
    segments = total // seg
    size = 4 * tokens + META
    scale = width ** (-0.5)
    factor = scale * LOG2E
    lane1 = lax.broadcasted_iota(jnp.int32, (1, tokens), 1)
    left = lane1 < seg

    places = []
    for ref, count in zip(blocks, counts):
        for index in range(count):
            base = index * size
            meta = ref[base + 4 * tokens : base + size].astype(jnp.float32)
            gate = (meta[0:1] + meta[1:2]) + meta[2:3]
            place = meta[3:4].astype(jnp.int32)
            pair = (place[0, 0], place[0, seg])
            places.append((ref, base, pair))
            for half in range(2):
                at = pl.multiple_of(pair[half] * seg, seg)
                for slot, dest in enumerate((qs, ks)):
                    first = base + slot * tokens + half * seg
                    dest[pl.ds(at, seg), :] = ref[first : first + seg, :]
                shifted = gate if half == 0 else pltpu.roll(gate, seg, 1)
                cums[pl.ds(pair[half], 1), :] = jnp.where(left, shifted, 0.0)
    own_place = places[0][2]

    inside = sum_lanes(cums[...], False)
    whole = jnp.broadcast_to(inside[:, seg - 1 : seg], inside.shape)
    before = roll_sum_rows(whole, False) - whole
    cums[...] = (inside + before) * LOG2E
    for tile in range(segments // 2):
        even = cums[2 * tile : 2 * tile + 1, :]
        odd = pltpu.roll(cums[2 * tile + 1 : 2 * tile + 2, :], seg, 1)
        key_row[:, tile * tokens : (tile + 1) * tokens] = jnp.where(left, even, odd)

    for ref, base, pair in places:
        for half in range(2):
            at = pl.multiple_of(pair[half] * seg, seg)
            for slot, dest in ((2, vs), (3, gs)):
                first = base + slot * tokens + half * seg
                dest[pl.ds(at, seg), :] = ref[first : first + seg, :]

    points[...] = jnp.zeros_like(points)
    inner = lax.broadcasted_iota(jnp.int32, (tokens, 1), 0)
    own = blocks[0]

    other = blocks[partner]
    pair_k = jnp.concatenate([own[tokens : 2 * tokens, :], other[tokens : 2 * tokens, :]], axis=0)
    pair_v = jnp.concatenate(
        [own[2 * tokens : 3 * tokens, :], other[2 * tokens : 3 * tokens, :]], axis=0
    )
    firsts = [0, sum(counts[:partner])]
    pair_key, pair_pos = [], []
    for first in firsts:
        place = places[first][2]
        key = [cums[pl.ds(p, 1), :] for p in place]
        pair_key.append(jnp.where(left, key[0], pltpu.roll(key[1], seg, 1)))
        pair_pos.append(
            jnp.where(left, place[0] * seg + lane1, place[1] * seg + lane1 - seg)
        )
    pair_key = jnp.concatenate(pair_key, axis=1)
    pair_pos = jnp.concatenate(pair_pos, axis=1)

    rows, cols = tokens, 2 * tokens
    steps = total // cols
    core = core_ref[0, 0]
    row_in = lax.broadcasted_iota(jnp.int32, (rows, cols), 0) + core * rows
    col_in = lax.broadcasted_iota(jnp.int32, (rows, cols), 1)
    causal = col_in <= row_in
    state = {}

    def open_item(item):
        r0 = pl.multiple_of((2 * item + core) * rows, rows)
        state[item] = dict(
            q=qs[pl.ds(r0, rows), :], g=gs[pl.ds(r0, rows), :], r0=r0, tiles=item + 1,
            s=[], p=[], low=[],
        )

    def score_tile(item, tile):
        it = state[item]
        s = score_of(it["q"], ks, key_row, tile, cols, factor)
        if tile == item:
            s = jnp.where(causal, s, masked_value)
        it["s"] += halves(s, width)

    def prob_tile(item, tile):
        it = state[item]
        for s in it["s"][2 * tile : 2 * tile + 2]:
            p = jnp.exp2(s - it["total"])
            it["p"].append(p)
            it["low"].append(p.astype(jnp.bfloat16))

    def outputs(item):
        it = state[item]
        out = jnp.dot(
            jnp.concatenate(it["low"], axis=1),
            vs[: it["tiles"] * cols, :],
            preferred_element_type=jnp.float32,
        )
        g = it["g"].astype(jnp.float32)
        it["delta"] = spread(jnp.sum(g * out, axis=1, keepdims=True), width)

    sums = dict(k=jnp.zeros((cols, width), jnp.float32), v=jnp.zeros((cols, width), jnp.float32))

    def pair_columns(item):
        it = state[item]
        s = contract_last(it["q"], pair_k) * factor - pair_key
        seen = pair_pos <= it["r0"] + inner
        p = jnp.where(seen, jnp.exp2(s - jnp.concatenate([it["total"]] * 2, axis=1)), 0.0)
        ds = p * (contract_last(it["g"], pair_v) - jnp.concatenate([it["delta"]] * 2, axis=1))
        sums["v"] = sums["v"] + contract_first(p.astype(jnp.bfloat16), it["g"])
        sums["k"] = sums["k"] + contract_first(ds.astype(jnp.bfloat16), it["q"])

    def last_stage(item):
        it = state[item]
        for tile in range(it["tiles"]):
            c0 = tile * cols
            dp = halves(contract_last(it["g"], vs[c0 : c0 + cols, :]), width)
            for at in range(2):
                ds = it["p"][2 * tile + at] * (dp[at] - it["delta"])
                first = c0 + at * width
                points[:, first : first + width] += jnp.sum(
                    ds.reshape(rows // 8, 8, width), axis=0
                )
        pair_columns(item)

    order = block_order(steps)
    open_item(order[0])
    for tile in range(state[order[0]]["tiles"]):
        score_tile(order[0], tile)
    state[order[0]]["total"] = log_total_of(state[order[0]]["s"], width)
    start_rows(own, own_place, ks, key_row, own_s, own_total)
    for turn, item in enumerate(order):
        after = order[turn + 1] if turn + 1 < len(order) else None
        here = list(range(state[item]["tiles"]))
        ahead = []
        if after is not None:
            open_item(after)
            ahead = list(range(state[after]["tiles"]))
        count = max(len(here), len(ahead))
        for at in range(count):
            for tile in split(ahead, at, count):
                score_tile(after, tile)
            for tile in split(here, at, count):
                prob_tile(item, tile)
        outputs(item)
        if after is not None:
            state[after]["total"] = log_total_of(state[after]["s"], width)
        last_stage(item)

    for tile in range(total // width):
        lines[tile : tile + 1, :] = -jnp.sum(
            points[:, tile * width : (tile + 1) * width], axis=0, keepdims=True
        )
    inside = sum_lanes(lines[...], True)
    whole = jnp.broadcast_to(inside[:, 0:1], inside.shape)
    lines[...] = inside + (roll_sum_rows(whole, True) - whole)
    for index, ref in enumerate((keep_ref, send_ref)):
        ref[0:tokens, :] = sums["k"][index * tokens : (index + 1) * tokens, :] * scale
        ref[tokens : 2 * tokens, :] = sums["v"][index * tokens : (index + 1) * tokens, :]
        parts = []
        for half, place in enumerate(places[firsts[index]][2]):
            line = lines[pl.ds(place // 2, 1), :]
            parts.append(jnp.where(place % 2 == half, line, pltpu.roll(line, seg, 1)))
        ref[2 * tokens : 2 * tokens + 8, :] = jnp.broadcast_to(
            jnp.where(left, parts[0], parts[1]), (8, width)
        )


def join_kernel(keep_ref, got_ref, dk_ref, dv_ref, gate_ref):
    tokens = dk_ref.shape[0]
    dk_ref[...] = keep_ref[0:tokens, :] + got_ref[0:tokens, :]
    dv_ref[...] = keep_ref[tokens : 2 * tokens, :] + got_ref[tokens : 2 * tokens, :]
    gate_ref[...] = keep_ref[2 * tokens : 2 * tokens + 1, :] + got_ref[2 * tokens : 2 * tokens + 1, :]


def core_call(blocks, tokens, width, devices, core, partner):
    size = 4 * tokens + META
    counts = tuple(b.shape[0] // size for b in blocks)
    total = tokens * devices
    segments = 2 * devices
    vmem = pl.BlockSpec(memory_space=pltpu.VMEM)
    smem = pl.BlockSpec(memory_space=pltpu.SMEM)
    part = jax.ShapeDtypeStruct((2 * tokens + 8, width), jnp.float32)
    sorted_rows = jax.ShapeDtypeStruct((total, width), jnp.bfloat16)
    return pl.pallas_call(
        functools.partial(core_kernel, counts, partner, tokens, width),
        out_shape=(
            part,
            part,
            sorted_rows,
            sorted_rows,
            jax.ShapeDtypeStruct((tokens, total), jnp.float32),
            jax.ShapeDtypeStruct((tokens, width), jnp.float32),
        ),
        in_specs=[smem] + [vmem] * len(blocks),
        out_specs=[vmem] * 6,
        scratch_shapes=[
            pltpu.VMEM((total, width), jnp.bfloat16),
            pltpu.VMEM((total, width), jnp.bfloat16),
            pltpu.VMEM((segments, tokens), jnp.float32),
            pltpu.VMEM((1, total), jnp.float32),
            pltpu.VMEM((8, total), jnp.float32),
            pltpu.VMEM((total // width, width), jnp.float32),
        ],
        compiler_params=pltpu.CompilerParams(vmem_limit_bytes=40 * 2**20),
        name="core",
    )(core, *blocks)


def row_call(own, ks, vs, own_s, own_total, tokens, width):
    vmem = pl.BlockSpec(memory_space=pltpu.VMEM)
    return pl.pallas_call(
        row_kernel,
        out_shape=(
            jax.ShapeDtypeStruct((tokens, width), jnp.bfloat16),
            jax.ShapeDtypeStruct((tokens, width), jnp.float32),
        ),
        in_specs=[vmem] * 5,
        out_specs=[vmem] * 2,
        compiler_params=pltpu.CompilerParams(vmem_limit_bytes=24 * 2**20),
        cost_estimate=pl.CostEstimate(
            flops=6 * tokens * ks.shape[0] * width,
            bytes_accessed=4 * ks.shape[0] * width,
            transcendentals=tokens * ks.shape[0],
        ),
        name="rows",
    )(own, ks, vs, own_s, own_total)


def join_call(keep, got, tokens, width):
    vmem = pl.BlockSpec(memory_space=pltpu.VMEM)
    square = jax.ShapeDtypeStruct((tokens, width), jnp.float32)
    return pl.pallas_call(
        join_kernel,
        out_shape=(square, square, jax.ShapeDtypeStruct((1, width), jnp.float32)),
        in_specs=[vmem, vmem],
        out_specs=[vmem] * 3,
        compiler_params=pltpu.CompilerParams(vmem_limit_bytes=2 * 2**20),
        name="join",
    )(keep, got)


def shift(x, devices, ring=0, flip=0):
    line = devices // 4
    walk = [0] + list(range(1, line, 2)) + list(range(2, line, 2))[::-1]
    pairs = []
    for step, place in enumerate(walk):
        target = walk[(step + ring) % line]
        pairs += [(place * 4 + low, target * 4 + (low ^ flip)) for low in range(4)]
    return lax.ppermute(x, "seq", pairs)


MOVES = (
    ("down", "down", "own"),
    ("up", "up", "own"),
    ("own_core", "core", "own"),
    ("side", "side", "own"),
    ("down_down", "down", "down"),
    ("down_side", "side", "down"),
    ("side_up", "up", "side"),
    ("up_core", "core", "up"),
    ("last", "side", "down_down"),
    ("down_core", "core", "down"),
    ("down_side_core", "core", "down_side"),
    ("side_core", "core", "side"),
    ("side_up_core", "core", "side_up"),
    ("down_down_core", "core", "down_down"),
    ("last_core", "core", "last"),
)
KINDS = {"up": {"ring": 1}, "down": {"ring": -1}, "side": {"flip": 2}, "core": {"flip": 1}}


def gather_blocks(x, devices):
    blocks = {"own": x}
    for name, kind, sent in MOVES:
        blocks[name] = shift(blocks[sent], devices, **KINDS[kind])
    return list(blocks.values())


def local_small(queries, keys, values, log_gate, out_grad, segment_order):
    tokens, width = queries.shape
    devices = lax.axis_size("seq")
    vmem = pl.BlockSpec(memory_space=pltpu.VMEM)
    packed = pl.pallas_call(
        pack_kernel,
        out_shape=jax.ShapeDtypeStruct((4 * tokens + META, width), jnp.bfloat16),
        in_specs=[pl.BlockSpec(memory_space=pltpu.HBM)] * 6,
        out_specs=vmem,
        scratch_shapes=[
            pltpu.VMEM((1, tokens), jnp.float32),
            pltpu.VMEM((1, 2), jnp.int32),
            pltpu.SemaphoreType.DMA((6,)),
        ],
        compiler_params=pltpu.CompilerParams(vmem_limit_bytes=2 * 2**20),
        name="pack",
    )(*[pltpu.with_memory_space_constraint(t, pltpu.HBM) for t in (queries, keys, values, out_grad, log_gate.reshape(1, tokens), segment_order.reshape(1, 2))])
    blocks = gather_blocks(packed, devices)
    core = (lax.axis_index("seq") % 2).astype(jnp.int32).reshape(1, 1)
    partner = 1 + [m[0] for m in MOVES].index("own_core")
    keep, send, ks, vs, own_s, own_total = core_call(blocks, tokens, width, devices, core, partner)
    got = shift(send, devices, flip=1)
    out, dq = row_call(packed, ks, vs, own_s, own_total, tokens, width)
    dk, dv, gate = join_call(keep, got, tokens, width)
    return (out, dq, dk, dv, gate.reshape(tokens))


def local(queries, keys, values, log_gate, out_grad, segment_order):
    tokens, width = queries.shape
    small = tokens == width and lax.axis_size("seq") == len(MOVES) + 1
    path = local_small if small else local_general
    return path(queries, keys, values, log_gate, out_grad, segment_order)


def solution(mesh):
    placed = (
        P(("grp", "seq"), None),
        P(("grp", "seq"), None),
        P(("grp", "seq"), None),
        P(("grp", "seq")),
        P(("grp", "seq"), None),
        P(("grp", "seq")),
    )
    return jax.shard_map(
        local,
        mesh=mesh,
        in_specs=placed,
        out_specs=(
            P(("grp", "seq"), None),
            P(("grp", "seq"), None),
            P(("grp", "seq"), None),
            P(("grp", "seq"), None),
            P(("grp", "seq")),
        ),
        check_vma=False,
    )
```

profile of v0, /device:TPU:0, one launch (start us, length us, event | category | flops | bytes accessed | tf_op | source)
XLA Modules:
  0.0 31.8 jit_solution(11973206863436574843)
XLA Ops:
  0.6 0.9 %pack.1.refs_0_.own = bf16[528,128]{1,0:T(8,128)(2,1)S(1)} custom-call(bf16[128,128]{1,0:T(8,128)(2,1)} %q_ref.1, bf16[128,128]{1,0:T(8,128)(2,1)} %k_ref.1, bf16[128,128]{1,0:T(8,128)(2,1)} %v_ref.1, bf16[128,128]{1,0:T(8,128)(2,1)} %g_ref.1, f32[1,128]{1,0:T(1,128)} %bitcast.4, s32[1,2]{1,0:T(1,128)} %bitcast.5), custom_call_target="tpu_custom_call" | custom-call | tf_op jit(solution)/shard_map/pack/pallas_call | solution.py:593
  1.5 4.1 %collective-permute-start = (bf16[528,128]{1,0:T(8,128)(2,1)S(1)}, bf16[528,128]{1,0:T(8,128)(2,1)S(1)}, u32[]{:S(2)}, u32[]{:S(2)}) collective-permute-start(bf16[528,128]{1,0:T(8,128)(2,1)S(1)} %pack.1.refs_0_.own), channel_id=1, source_target_pairs={{0,8},{1,9},{2,10},{3,11},{4,0},{5,1},{6,2},{7,3},{12,4},{13,5},{1... | collective-permute-start | bytes 405512 | tf_op jit(solution)/shard_map/ppermute | solution.py:559
  5.6 1.5 %collective-permute-start.3 = (bf16[528,128]{1,0:T(8,128)(2,1)S(1)}, bf16[528,128]{1,0:T(8,128)(2,1)S(1)}, u32[]{:S(2)}, u32[]{:S(2)}) collective-permute-start(bf16[528,128]{1,0:T(8,128)(2,1)S(1)} %pack.1.refs_0_.own), channel_id=1, source_target_pairs={{0,2},{1,3},{2,0},{3,1},{4,6},{5,7},{6,4},{7,5},{12,14},{13,15},{1... | collective-permute-start | bytes 405512 | tf_op jit(solution)/shard_map/ppermute | solution.py:559
  7.1 0.0 collective-permute-start.1
  7.1 0.0 collective-permute-start.2
  7.1 2.5 %collective-permute-done.refs_1_ = bf16[528,128]{1,0:T(8,128)(2,1)S(1)} collective-permute-done((bf16[528,128]{1,0:T(8,128)(2,1)S(1)}, bf16[528,128]{1,0:T(8,128)(2,1)S(1)}, u32[]{:S(2)}, u32[]{:S(2)}) %collective-permute-start) | collective-permute-done | bytes 135200 | tf_op jit(solution)/shard_map/ppermute | solution.py:559
  9.6 3.4 %collective-permute-start.4 = (bf16[528,128]{1,0:T(8,128)(2,1)S(1)}, bf16[528,128]{1,0:T(8,128)(2,1)S(1)}, u32[]{:S(2)}, u32[]{:S(2)}) collective-permute-start(bf16[528,128]{1,0:T(8,128)(2,1)S(1)} %collective-permute-done.refs_1_), channel_id=1, source_target_pairs={{0,8},{1,9},{2,10},{3,11},{4,0},{5,1},{6,2},{7,3},{12,4},{13,5},{1... | collective-permute-start | bytes 405512 | tf_op jit(solution)/shard_map/ppermute | solution.py:559
  13.0 0.0 collective-permute-done.3.refs_4_
  13.0 0.0 collective-permute-start.11
  13.0 0.0 collective-permute-start.6
  13.0 0.7 %collective-permute-done.1.refs_2_ = bf16[528,128]{1,0:T(8,128)(2,1)S(1)} collective-permute-done((bf16[528,128]{1,0:T(8,128)(2,1)S(1)}, bf16[528,128]{1,0:T(8,128)(2,1)S(1)}, u32[]{:S(2)}, u32[]{:S(2)}) %collective-permute-start.1) | collective-permute-done | bytes 135200 | tf_op jit(solution)/shard_map/ppermute | solution.py:559
  13.7 0.0 collective-permute-start.7
  13.7 0.0 collective-permute-done.2.refs_3_
  13.7 1.5 %collective-permute-start.5 = (bf16[528,128]{1,0:T(8,128)(2,1)S(1)}, bf16[528,128]{1,0:T(8,128)(2,1)S(1)}, u32[]{:S(2)}, u32[]{:S(2)}) collective-permute-start(bf16[528,128]{1,0:T(8,128)(2,1)S(1)} %collective-permute-done.refs_1_), channel_id=1, source_target_pairs={{0,2},{1,3},{2,0},{3,1},{4,6},{5,7},{6,4},{7,5},{12,14},{13,15},{1... | collective-permute-start | bytes 405512 | tf_op jit(solution)/shard_map/ppermute | solution.py:559
  15.2 1.6 %collective-permute-done.4.refs_5_ = bf16[528,128]{1,0:T(8,128)(2,1)S(1)} collective-permute-done((bf16[528,128]{1,0:T(8,128)(2,1)S(1)}, bf16[528,128]{1,0:T(8,128)(2,1)S(1)}, u32[]{:S(2)}, u32[]{:S(2)}) %collective-permute-start.4) | collective-permute-done | bytes 135200 | tf_op jit(solution)/shard_map/ppermute | solution.py:559
  16.8 1.5 %collective-permute-start.8 = (bf16[528,128]{1,0:T(8,128)(2,1)S(1)}, bf16[528,128]{1,0:T(8,128)(2,1)S(1)}, u32[]{:S(2)}, u32[]{:S(2)}) collective-permute-start(bf16[528,128]{1,0:T(8,128)(2,1)S(1)} %collective-permute-done.4.refs_5_), channel_id=1, source_target_pairs={{0,2},{1,3},{2,0},{3,1},{4,6},{5,7},{6,4},{7,5},{12,14},{13,15},{1... | collective-permute-start | bytes 405512 | tf_op jit(solution)/shard_map/ppermute | solution.py:559
  18.3 0.0 collective-permute-done.11.refs_12_
  18.3 0.0 collective-permute-start.9
  18.3 1.8 %collective-permute-done.6.refs_7_ = bf16[528,128]{1,0:T(8,128)(2,1)S(1)} collective-permute-done((bf16[528,128]{1,0:T(8,128)(2,1)S(1)}, bf16[528,128]{1,0:T(8,128)(2,1)S(1)}, u32[]{:S(2)}, u32[]{:S(2)}) %collective-permute-start.6) | collective-permute-done | bytes 135200 | tf_op jit(solution)/shard_map/ppermute | solution.py:559
  20.1 0.0 collective-permute-start.13
  20.1 0.0 collective-permute-done.7.refs_8_
  20.1 0.5 %collective-permute-start.12 = (bf16[528,128]{1,0:T(8,128)(2,1)S(1)}, bf16[528,128]{1,0:T(8,128)(2,1)S(1)}, u32[]{:S(2)}, u32[]{:S(2)}) collective-permute-start(bf16[528,128]{1,0:T(8,128)(2,1)S(1)} %collective-permute-done.6.refs_7_), channel_id=1, source_target_pairs={{0,1},{1,0},{2,3},{3,2},{4,5},{5,4},{6,7},{7,6},{12,13},{13,12},{1... | collective-permute-start | bytes 405512 | tf_op jit(solution)/shard_map/ppermute | solution.py:559
  20.6 0.0 collective-permute-done.5.refs_6_
  20.6 0.1 collective-permute-start.10
  20.7 1.9 %collective-permute-done.8.refs_9_ = bf16[528,128]{1,0:T(8,128)(2,1)S(1)} collective-permute-done((bf16[528,128]{1,0:T(8,128)(2,1)S(1)}, bf16[528,128]{1,0:T(8,128)(2,1)S(1)}, u32[]{:S(2)}, u32[]{:S(2)}) %collective-permute-start.8) | collective-permute-done | bytes 135200 | tf_op jit(solution)/shard_map/ppermute | solution.py:559
  22.6 0.0 collective-permute-start.14
  22.6 0.0 collective-permute-done.9.refs_10_
  22.6 0.0 collective-permute-done.12.refs_13_
  22.6 0.0 collective-permute-done.10.refs_11_
  22.6 0.0 collective-permute-done.13.refs_14_
  22.6 1.3 %collective-permute-done.14.refs_15_ = bf16[528,128]{1,0:T(8,128)(2,1)S(1)} collective-permute-done((bf16[528,128]{1,0:T(8,128)(2,1)S(1)}, bf16[528,128]{1,0:T(8,128)(2,1)S(1)}, u32[]{:S(2)}, u32[]{:S(2)}) %collective-permute-start.14) | collective-permute-done | bytes 135200 | tf_op jit(solution)/shard_map/ppermute | solution.py:559
  23.9 5.5 %core.1 = (f32[264,128]{1,0:T(8,128)S(1)}, f32[264,128]{1,0:T(8,128)S(1)}, bf16[2048,128]{1,0:T(8,128)(2,1)S(1)}, bf16[2048,128]{1,0:T(8,128)(2,1)S(1)}, f32[128...) custom-call(s32[1,1]{1,0:T(1,128)} %bitcast.2.core_ref, bf16[528,128]{1,0:T(8,128)(2,1)S(1)} %pack.1.refs_0_.own, ...), custom_call_target="tpu_custom_call" | custom-call | tf_op jit(solution)/shard_map/core/pallas_call | solution.py:494
  29.5 0.2 collective-permute-start.15
  29.7 1.4 %rows.1 = (bf16[128,128]{1,0:T(8,128)(2,1)}, f32[128,128]{1,0:T(8,128)}) custom-call(bf16[528,128]{1,0:T(8,128)(2,1)S(1)} %pack.1.refs_0_.own, bf16[2048,128]{1,0:T(8,128)(2,1)S(1)} %get-tuple-element.16.ks, bf16[2048,128]{1,0:T(8,128)(2,1)S(1)} %get-tuple-element.17.vs, f32[128,2048]{1,0:T(8,128)S(1)} %get-tuple-element.18.own_s, ...), custom_call_target="tpu_custom_call" | custom-call | flops 201326592 | bytes 1048576 | tf_op jit(solution)/shard_map/rows/pallas_call | solution.py:521
  31.1 0.0 collective-permute-done.15.got_ref
  31.1 0.7 %join.1 = (f32[128,128]{1,0:T(8,128)}, f32[128,128]{1,0:T(8,128)}, f32[1,128]{1,0:T(1,128)}) custom-call(f32[264,128]{1,0:T(8,128)S(1)} %get-tuple-element.22.keep_ref, f32[264,128]{1,0:T(8,128)S(1)} %collective-permute-done.15.got_ref), custom_call_target="tpu_custom_call" | custom-call | tf_op jit(solution)/shard_map/join/pallas_call | solution.py:542
Async XLA Ops:
  1.5 8.1 %collective-permute-start = (bf16[528,128]{1,0:T(8,128)(2,1)S(1)}, bf16[528,128]{1,0:T(8,128)(2,1)S(1)}, u32[]{:S(2)}, u32[]{:S(2)}) collective-permute-start(bf16[528,128]{1,0:T(8,128)(2,1)S(1)} %pack.1.refs_0_.own), channel_id=1, source_target_pairs={{0,8},{1,9},{2,10},{3,11},{4,0},{5,1},{6,2},{7,3},{12,4},{13,5},{1... | collective-permute-start | bytes 405512 | tf_op jit(solution)/shard_map/ppermute | solution.py:559
  5.6 7.4 %collective-permute-start.3 = (bf16[528,128]{1,0:T(8,128)(2,1)S(1)}, bf16[528,128]{1,0:T(8,128)(2,1)S(1)}, u32[]{:S(2)}, u32[]{:S(2)}) collective-permute-start(bf16[528,128]{1,0:T(8,128)(2,1)S(1)} %pack.1.refs_0_.own), channel_id=1, source_target_pairs={{0,2},{1,3},{2,0},{3,1},{4,6},{5,7},{6,4},{7,5},{12,14},{13,15},{1... | collective-permute-start | bytes 405512 | tf_op jit(solution)/shard_map/ppermute | solution.py:559
  7.1 6.5 %collective-permute-start.1 = (bf16[528,128]{1,0:T(8,128)(2,1)S(1)}, bf16[528,128]{1,0:T(8,128)(2,1)S(1)}, u32[]{:S(2)}, u32[]{:S(2)}) collective-permute-start(bf16[528,128]{1,0:T(8,128)(2,1)S(1)} %pack.1.refs_0_.own), channel_id=1, source_target_pairs={{0,4},{1,5},{2,6},{3,7},{4,12},{5,13},{6,14},{7,15},{12,8},{13,9},... | collective-permute-start | bytes 405512 | tf_op jit(solution)/shard_map/ppermute | solution.py:559
  7.1 6.5 %collective-permute-start.2 = (bf16[528,128]{1,0:T(8,128)(2,1)S(1)}, bf16[528,128]{1,0:T(8,128)(2,1)S(1)}, u32[]{:S(2)}, u32[]{:S(2)}) collective-permute-start(bf16[528,128]{1,0:T(8,128)(2,1)S(1)} %pack.1.refs_0_.own), channel_id=1, source_target_pairs={{0,1},{1,0},{2,3},{3,2},{4,5},{5,4},{6,7},{7,6},{12,13},{13,12},{1... | collective-permute-start | bytes 405512 | tf_op jit(solution)/shard_map/ppermute | solution.py:559
  9.6 7.2 %collective-permute-start.4 = (bf16[528,128]{1,0:T(8,128)(2,1)S(1)}, bf16[528,128]{1,0:T(8,128)(2,1)S(1)}, u32[]{:S(2)}, u32[]{:S(2)}) collective-permute-start(bf16[528,128]{1,0:T(8,128)(2,1)S(1)} %collective-permute-done.refs_1_), channel_id=1, source_target_pairs={{0,8},{1,9},{2,10},{3,11},{4,0},{5,1},{6,2},{7,3},{12,4},{13,5},{1... | collective-permute-start | bytes 405512 | tf_op jit(solution)/shard_map/ppermute | solution.py:559
  13.0 5.3 %collective-permute-start.11 = (bf16[528,128]{1,0:T(8,128)(2,1)S(1)}, bf16[528,128]{1,0:T(8,128)(2,1)S(1)}, u32[]{:S(2)}, u32[]{:S(2)}) collective-permute-start(bf16[528,128]{1,0:T(8,128)(2,1)S(1)} %collective-permute-done.3.refs_4_), channel_id=1, source_target_pairs={{0,1},{1,0},{2,3},{3,2},{4,5},{5,4},{6,7},{7,6},{12,13},{13,12},{1... | collective-permute-start | bytes 405512 | tf_op jit(solution)/shard_map/ppermute | solution.py:559
  13.0 7.1 %collective-permute-start.6 = (bf16[528,128]{1,0:T(8,128)(2,1)S(1)}, bf16[528,128]{1,0:T(8,128)(2,1)S(1)}, u32[]{:S(2)}, u32[]{:S(2)}) collective-permute-start(bf16[528,128]{1,0:T(8,128)(2,1)S(1)} %collective-permute-done.3.refs_4_), channel_id=1, source_target_pairs={{0,4},{1,5},{2,6},{3,7},{4,12},{5,13},{6,14},{7,15},{12,8},{13,9},... | collective-permute-start | bytes 405512 | tf_op jit(solution)/shard_map/ppermute | solution.py:559
  13.7 6.4 %collective-permute-start.7 = (bf16[528,128]{1,0:T(8,128)(2,1)S(1)}, bf16[528,128]{1,0:T(8,128)(2,1)S(1)}, u32[]{:S(2)}, u32[]{:S(2)}) collective-permute-start(bf16[528,128]{1,0:T(8,128)(2,1)S(1)} %collective-permute-done.1.refs_2_), channel_id=1, source_target_pairs={{0,1},{1,0},{2,3},{3,2},{4,5},{5,4},{6,7},{7,6},{12,13},{13,12},{1... | collective-permute-start | bytes 405512 | tf_op jit(solution)/shard_map/ppermute | solution.py:559
  13.7 6.9 %collective-permute-start.5 = (bf16[528,128]{1,0:T(8,128)(2,1)S(1)}, bf16[528,128]{1,0:T(8,128)(2,1)S(1)}, u32[]{:S(2)}, u32[]{:S(2)}) collective-permute-start(bf16[528,128]{1,0:T(8,128)(2,1)S(1)} %collective-permute-done.refs_1_), channel_id=1, source_target_pairs={{0,2},{1,3},{2,0},{3,1},{4,6},{5,7},{6,4},{7,5},{12,14},{13,15},{1... | collective-permute-start | bytes 405512 | tf_op jit(solution)/shard_map/ppermute | solution.py:559
  16.8 5.8 %collective-permute-start.8 = (bf16[528,128]{1,0:T(8,128)(2,1)S(1)}, bf16[528,128]{1,0:T(8,128)(2,1)S(1)}, u32[]{:S(2)}, u32[]{:S(2)}) collective-permute-start(bf16[528,128]{1,0:T(8,128)(2,1)S(1)} %collective-permute-done.4.refs_5_), channel_id=1, source_target_pairs={{0,2},{1,3},{2,0},{3,1},{4,6},{5,7},{6,4},{7,5},{12,14},{13,15},{1... | collective-permute-start | bytes 405512 | tf_op jit(solution)/shard_map/ppermute | solution.py:559
  18.3 4.3 %collective-permute-start.9 = (bf16[528,128]{1,0:T(8,128)(2,1)S(1)}, bf16[528,128]{1,0:T(8,128)(2,1)S(1)}, u32[]{:S(2)}, u32[]{:S(2)}) collective-permute-start(bf16[528,128]{1,0:T(8,128)(2,1)S(1)} %collective-permute-done.refs_1_), channel_id=1, source_target_pairs={{0,1},{1,0},{2,3},{3,2},{4,5},{5,4},{6,7},{7,6},{12,13},{13,12},{1... | collective-permute-start | bytes 405512 | tf_op jit(solution)/shard_map/ppermute | solution.py:559
  20.1 2.5 %collective-permute-start.13 = (bf16[528,128]{1,0:T(8,128)(2,1)S(1)}, bf16[528,128]{1,0:T(8,128)(2,1)S(1)}, u32[]{:S(2)}, u32[]{:S(2)}) collective-permute-start(bf16[528,128]{1,0:T(8,128)(2,1)S(1)} %collective-permute-done.4.refs_5_), channel_id=1, source_target_pairs={{0,1},{1,0},{2,3},{3,2},{4,5},{5,4},{6,7},{7,6},{12,13},{13,12},{1... | collective-permute-start | bytes 405512 | tf_op jit(solution)/shard_map/ppermute | solution.py:559
  20.1 2.5 %collective-permute-start.12 = (bf16[528,128]{1,0:T(8,128)(2,1)S(1)}, bf16[528,128]{1,0:T(8,128)(2,1)S(1)}, u32[]{:S(2)}, u32[]{:S(2)}) collective-permute-start(bf16[528,128]{1,0:T(8,128)(2,1)S(1)} %collective-permute-done.6.refs_7_), channel_id=1, source_target_pairs={{0,1},{1,0},{2,3},{3,2},{4,5},{5,4},{6,7},{7,6},{12,13},{13,12},{1... | collective-permute-start | bytes 405512 | tf_op jit(solution)/shard_map/ppermute | solution.py:559
  20.6 2.0 %collective-permute-start.10 = (bf16[528,128]{1,0:T(8,128)(2,1)S(1)}, bf16[528,128]{1,0:T(8,128)(2,1)S(1)}, u32[]{:S(2)}, u32[]{:S(2)}) collective-permute-start(bf16[528,128]{1,0:T(8,128)(2,1)S(1)} %collective-permute-done.5.refs_6_), channel_id=1, source_target_pairs={{0,1},{1,0},{2,3},{3,2},{4,5},{5,4},{6,7},{7,6},{12,13},{13,12},{1... | collective-permute-start | bytes 405512 | tf_op jit(solution)/shard_map/ppermute | solution.py:559
  22.6 1.4 %collective-permute-start.14 = (bf16[528,128]{1,0:T(8,128)(2,1)S(1)}, bf16[528,128]{1,0:T(8,128)(2,1)S(1)}, u32[]{:S(2)}, u32[]{:S(2)}) collective-permute-start(bf16[528,128]{1,0:T(8,128)(2,1)S(1)} %collective-permute-done.8.refs_9_), channel_id=1, source_target_pairs={{0,1},{1,0},{2,3},{3,2},{4,5},{5,4},{6,7},{7,6},{12,13},{13,12},{1... | collective-permute-start | bytes 405512 | tf_op jit(solution)/shard_map/ppermute | solution.py:559
  29.5 1.7 %collective-permute-start.15 = (f32[264,128]{1,0:T(8,128)S(1)}, f32[264,128]{1,0:T(8,128)S(1)}, u32[]{:S(2)}, u32[]{:S(2)}) collective-permute-start(f32[264,128]{1,0:T(8,128)S(1)} %get-tuple-element.23), channel_id=1, source_target_pairs={{0,1},{1,0},{2,3},{3,2},{4,5},{5,4},{6,7},{7,6},{12,13},{13,12},{1... | collective-permute-start | bytes 405512 | tf_op jit(solution)/shard_map/ppermute | solution.py:559
where the time goes:
time: 32 us; the launch traced here: 31.8 us
  starting transfers between devices  12.8 us (40%)
  waiting for transfers between devices  9.78 us (31%)
  Pallas kernels  8.55 us (27%)
  between operations  0.69 us (2%)
    ppermute x16, starting transfers between devices, shift(): return lax.ppermute(x, 'seq', pairs)  12.8 us
    ppermute x16, waiting for transfers between devices, shift(): return lax.ppermute(x, 'seq', pairs)  9.78 us
    pallas_call x1, Pallas kernels, core_call(): pl.pallas_call(functools.partial(core_kernel, counts, partner, tokens, wi...  5.55 us
    pallas_call x1, Pallas kernels, row_call(): pl.pallas_call(row_kernel, out_shape=(jax.ShapeDtypeStruct((tokens, width...  1.45 us
    pallas_call x1, Pallas kernels, local_small(): pl.pallas_call(pack_kernel, out_shape=jax.ShapeDtypeStruct((4 * tokens +...  0.89 us
    pallas_call x1, Pallas kernels, join_call(): pl.pallas_call(join_kernel, out_shape=(square, square, jax.ShapeDtypeStru...  0.67 us
  transfers between devices with their start and end apart: 16, of which 6 were waited for; matrix products, arithmetic and copies ran while one was open for 0% of the time, Pallas kernels for 5%

commit v1 on v0

--- a/solution.py
+++ b/solution.py
@@ -475,8 +475,10 @@
         )
 
 
-def join_kernel(keep_ref, got_ref, dk_ref, dv_ref, gate_ref):
+def join_kernel(keep_ref, got_ref, rows_out, rows_dq, dk_ref, dv_ref, gate_ref, out_ref, dq_ref):
     tokens = dk_ref.shape[0]
+    out_ref[...] = rows_out[...]
+    dq_ref[...] = rows_dq[...]
     dk_ref[...] = keep_ref[0:tokens, :] + got_ref[0:tokens, :]
     dv_ref[...] = keep_ref[tokens : 2 * tokens, :] + got_ref[tokens : 2 * tokens, :]
     gate_ref[...] = keep_ref[2 * tokens : 2 * tokens + 1, :] + got_ref[2 * tokens : 2 * tokens + 1, :]
@@ -536,17 +538,23 @@
     )(own, ks, vs, own_s, own_total)
 
 
-def join_call(keep, got, tokens, width):
+def join_call(keep, got, out, dq, tokens, width):
     vmem = pl.BlockSpec(memory_space=pltpu.VMEM)
     square = jax.ShapeDtypeStruct((tokens, width), jnp.float32)
     return pl.pallas_call(
         join_kernel,
-        out_shape=(square, square, jax.ShapeDtypeStruct((1, width), jnp.float32)),
-        in_specs=[vmem, vmem],
-        out_specs=[vmem] * 3,
+        out_shape=(
+            square,
+            square,
+            jax.ShapeDtypeStruct((1, width), jnp.float32),
+            jax.ShapeDtypeStruct((tokens, width), jnp.bfloat16),
+            square,
+        ),
+        in_specs=[vmem] * 4,
+        out_specs=[vmem] * 5,
         compiler_params=pltpu.CompilerParams(vmem_limit_bytes=2 * 2**20),
         name="join",
-    )(keep, got)
+    )(keep, got, out, dq)
 
 
 def shift(x, devices, ring=0, flip=0):
@@ -609,7 +617,7 @@
     keep, send, ks, vs, own_s, own_total = core_call(blocks, tokens, width, devices, core, partner)
     got = shift(send, devices, flip=1)
     out, dq = row_call(packed, ks, vs, own_s, own_total, tokens, width)
-    dk, dv, gate = join_call(keep, got, tokens, width)
+    dk, dv, gate, out, dq = join_call(keep, got, out, dq, tokens, width)
     return (out, dq, dk, dv, gate.reshape(tokens))
 
 

time: 32 us -> 31.8 us (level)
  Pallas kernels: 8.55 us -> 7.95 us
  waiting for transfers between devices: 9.78 us -> 10.2 us
    pallas_call x1, Pallas kernels: 1.45 us -> 0.81 us  [row_call(): pl.pallas_call(row_kernel, out_shape=(jax.ShapeDtypeStruct((tokens, width...]
    ppermute x16, waiting for transfers between devices: 9.78 us -> 10.2 us  [shift(): return lax.ppermute(x, 'seq', pairs)]
  transfers between devices with their start and end apart: 16 -> 16, of which waited for: 6 -> 7; matrix products, arithmetic and copies ran while one was open for 0% -> 0% of each run, Pallas kernels for 5% -> 3%
where the time goes in v1:
time: 31.8 us; the launch traced here: 31.6 us
  starting transfers between devices  12.8 us (40%)
  waiting for transfers between devices  10.2 us (32%)
  Pallas kernels  7.95 us (25%)
  between operations  0.7 us (2%)
    ppermute x16, starting transfers between devices, shift(): return lax.ppermute(x, 'seq', pairs)  12.8 us
    ppermute x16, waiting for transfers between devices, shift(): return lax.ppermute(x, 'seq', pairs)  10.2 us
    pallas_call x1, Pallas kernels, core_call(): pl.pallas_call(functools.partial(core_kernel, counts, partner, tokens, wi...  5.55 us
    pallas_call x1, Pallas kernels, local_small(): pl.pallas_call(pack_kernel, out_shape=jax.ShapeDtypeStruct((4 * tokens +...  0.89 us
    pallas_call x1, Pallas kernels, row_call(): pl.pallas_call(row_kernel, out_shape=(jax.ShapeDtypeStruct((tokens, width...  0.81 us
    pallas_call x1, Pallas kernels, join_call(): pl.pallas_call(join_kernel, out_shape=(square, square, jax.ShapeDtypeStru...  0.71 us
  transfers between devices with their start and end apart: 16, of which 7 were waited for; matrix products, arithmetic and copies ran while one was open for 0% of the time, Pallas kernels for 3%

profile of v1, /device:TPU:0, one launch (start us, length us, event | category | flops | bytes accessed | tf_op | source)
XLA Modules:
  0.0 31.6 jit_solution(12464015033926810659)
XLA Ops:
  0.6 0.9 %pack.1.refs_0_.own = bf16[528,128]{1,0:T(8,128)(2,1)S(1)} custom-call(bf16[128,128]{1,0:T(8,128)(2,1)} %q_ref.1, bf16[128,128]{1,0:T(8,128)(2,1)} %k_ref.1, bf16[128,128]{1,0:T(8,128)(2,1)} %v_ref.1, bf16[128,128]{1,0:T(8,128)(2,1)} %g_ref.1, f32[1,128]{1,0:T(1,128)} %bitcast.4, s32[1,2]{1,0:T(1,128)} %bitcast.5), custom_call_target="tpu_custom_call" | custom-call | tf_op jit(solution)/shard_map/pack/pallas_call | solution.py:601
  1.5 4.1 %collective-permute-start = (bf16[528,128]{1,0:T(8,128)(2,1)S(1)}, bf16[528,128]{1,0:T(8,128)(2,1)S(1)}, u32[]{:S(2)}, u32[]{:S(2)}) collective-permute-start(bf16[528,128]{1,0:T(8,128)(2,1)S(1)} %pack.1.refs_0_.own), channel_id=1, source_target_pairs={{0,8},{1,9},{2,10},{3,11},{4,0},{5,1},{6,2},{7,3},{12,4},{13,5},{1... | collective-permute-start | bytes 405512 | tf_op jit(solution)/shard_map/ppermute | solution.py:567
  5.6 1.5 %collective-permute-start.3 = (bf16[528,128]{1,0:T(8,128)(2,1)S(1)}, bf16[528,128]{1,0:T(8,128)(2,1)S(1)}, u32[]{:S(2)}, u32[]{:S(2)}) collective-permute-start(bf16[528,128]{1,0:T(8,128)(2,1)S(1)} %pack.1.refs_0_.own), channel_id=1, source_target_pairs={{0,2},{1,3},{2,0},{3,1},{4,6},{5,7},{6,4},{7,5},{12,14},{13,15},{1... | collective-permute-start | bytes 405512 | tf_op jit(solution)/shard_map/ppermute | solution.py:567
  7.1 0.0 collective-permute-start.1
  7.1 0.0 collective-permute-start.2
  7.1 2.5 %collective-permute-done.refs_1_ = bf16[528,128]{1,0:T(8,128)(2,1)S(1)} collective-permute-done((bf16[528,128]{1,0:T(8,128)(2,1)S(1)}, bf16[528,128]{1,0:T(8,128)(2,1)S(1)}, u32[]{:S(2)}, u32[]{:S(2)}) %collective-permute-start) | collective-permute-done | bytes 135200 | tf_op jit(solution)/shard_map/ppermute | solution.py:567
  9.6 3.4 %collective-permute-start.4 = (bf16[528,128]{1,0:T(8,128)(2,1)S(1)}, bf16[528,128]{1,0:T(8,128)(2,1)S(1)}, u32[]{:S(2)}, u32[]{:S(2)}) collective-permute-start(bf16[528,128]{1,0:T(8,128)(2,1)S(1)} %collective-permute-done.refs_1_), channel_id=1, source_target_pairs={{0,8},{1,9},{2,10},{3,11},{4,0},{5,1},{6,2},{7,3},{12,4},{13,5},{1... | collective-permute-start | bytes 405512 | tf_op jit(solution)/shard_map/ppermute | solution.py:567
  13.0 0.0 collective-permute-done.3.refs_4_
  13.0 0.0 collective-permute-start.11
  13.0 0.0 collective-permute-start.6
  13.0 0.7 %collective-permute-done.1.refs_2_ = bf16[528,128]{1,0:T(8,128)(2,1)S(1)} collective-permute-done((bf16[528,128]{1,0:T(8,128)(2,1)S(1)}, bf16[528,128]{1,0:T(8,128)(2,1)S(1)}, u32[]{:S(2)}, u32[]{:S(2)}) %collective-permute-start.1) | collective-permute-done | bytes 135200 | tf_op jit(solution)/shard_map/ppermute | solution.py:567
  13.7 0.0 collective-permute-start.7
  13.7 0.0 collective-permute-done.2.refs_3_
  13.7 1.5 %collective-permute-start.5 = (bf16[528,128]{1,0:T(8,128)(2,1)S(1)}, bf16[528,128]{1,0:T(8,128)(2,1)S(1)}, u32[]{:S(2)}, u32[]{:S(2)}) collective-permute-start(bf16[528,128]{1,0:T(8,128)(2,1)S(1)} %collective-permute-done.refs_1_), channel_id=1, source_target_pairs={{0,2},{1,3},{2,0},{3,1},{4,6},{5,7},{6,4},{7,5},{12,14},{13,15},{1... | collective-permute-start | bytes 405512 | tf_op jit(solution)/shard_map/ppermute | solution.py:567
  15.2 1.6 %collective-permute-done.4.refs_5_ = bf16[528,128]{1,0:T(8,128)(2,1)S(1)} collective-permute-done((bf16[528,128]{1,0:T(8,128)(2,1)S(1)}, bf16[528,128]{1,0:T(8,128)(2,1)S(1)}, u32[]{:S(2)}, u32[]{:S(2)}) %collective-permute-start.4) | collective-permute-done | bytes 135200 | tf_op jit(solution)/shard_map/ppermute | solution.py:567
  16.8 1.5 %collective-permute-start.8 = (bf16[528,128]{1,0:T(8,128)(2,1)S(1)}, bf16[528,128]{1,0:T(8,128)(2,1)S(1)}, u32[]{:S(2)}, u32[]{:S(2)}) collective-permute-start(bf16[528,128]{1,0:T(8,128)(2,1)S(1)} %collective-permute-done.4.refs_5_), channel_id=1, source_target_pairs={{0,2},{1,3},{2,0},{3,1},{4,6},{5,7},{6,4},{7,5},{12,14},{13,15},{1... | collective-permute-start | bytes 405512 | tf_op jit(solution)/shard_map/ppermute | solution.py:567
  18.3 0.0 collective-permute-done.11.refs_12_
  18.3 0.0 collective-permute-start.9
  18.3 1.8 %collective-permute-done.6.refs_7_ = bf16[528,128]{1,0:T(8,128)(2,1)S(1)} collective-permute-done((bf16[528,128]{1,0:T(8,128)(2,1)S(1)}, bf16[528,128]{1,0:T(8,128)(2,1)S(1)}, u32[]{:S(2)}, u32[]{:S(2)}) %collective-permute-start.6) | collective-permute-done | bytes 135200 | tf_op jit(solution)/shard_map/ppermute | solution.py:567
  20.1 0.0 collective-permute-start.13
  20.1 0.0 collective-permute-done.7.refs_8_
  20.1 0.5 %collective-permute-start.12 = (bf16[528,128]{1,0:T(8,128)(2,1)S(1)}, bf16[528,128]{1,0:T(8,128)(2,1)S(1)}, u32[]{:S(2)}, u32[]{:S(2)}) collective-permute-start(bf16[528,128]{1,0:T(8,128)(2,1)S(1)} %collective-permute-done.6.refs_7_), channel_id=1, source_target_pairs={{0,1},{1,0},{2,3},{3,2},{4,5},{5,4},{6,7},{7,6},{12,13},{13,12},{1... | collective-permute-start | bytes 405512 | tf_op jit(solution)/shard_map/ppermute | solution.py:567
  20.6 0.0 collective-permute-done.5.refs_6_
  20.6 0.1 collective-permute-start.10
  20.7 1.9 %collective-permute-done.8.refs_9_ = bf16[528,128]{1,0:T(8,128)(2,1)S(1)} collective-permute-done((bf16[528,128]{1,0:T(8,128)(2,1)S(1)}, bf16[528,128]{1,0:T(8,128)(2,1)S(1)}, u32[]{:S(2)}, u32[]{:S(2)}) %collective-permute-start.8) | collective-permute-done | bytes 135200 | tf_op jit(solution)/shard_map/ppermute | solution.py:567
  22.6 0.0 collective-permute-start.14
  22.6 0.0 collective-permute-done.9.refs_10_
  22.6 0.0 collective-permute-done.12.refs_13_
  22.6 0.0 collective-permute-done.10.refs_11_
  22.6 0.0 collective-permute-done.13.refs_14_
  22.6 1.3 %collective-permute-done.14.refs_15_ = bf16[528,128]{1,0:T(8,128)(2,1)S(1)} collective-permute-done((bf16[528,128]{1,0:T(8,128)(2,1)S(1)}, bf16[528,128]{1,0:T(8,128)(2,1)S(1)}, u32[]{:S(2)}, u32[]{:S(2)}) %collective-permute-start.14) | collective-permute-done | bytes 135200 | tf_op jit(solution)/shard_map/ppermute | solution.py:567
  23.9 5.5 %core.1 = (f32[264,128]{1,0:T(8,128)S(1)}, f32[264,128]{1,0:T(8,128)S(1)}, bf16[2048,128]{1,0:T(8,128)(2,1)S(1)}, bf16[2048,128]{1,0:T(8,128)(2,1)S(1)}, f32[128...) custom-call(s32[1,1]{1,0:T(1,128)} %bitcast.core_ref, bf16[528,128]{1,0:T(8,128)(2,1)S(1)} %pack.1.refs_0_.own, ...), custom_call_target="tpu_custom_call" | custom-call | tf_op jit(solution)/shard_map/core/pallas_call | solution.py:496
  29.5 0.2 collective-permute-start.15
  29.7 0.8 %rows.1 = (bf16[128,128]{1,0:T(8,128)(2,1)S(1)}, f32[128,128]{1,0:T(8,128)S(1)}) custom-call(bf16[528,128]{1,0:T(8,128)(2,1)S(1)} %pack.1.refs_0_.own, bf16[2048,128]{1,0:T(8,128)(2,1)S(1)} %get-tuple-element.20.ks, bf16[2048,128]{1,0:T(8,128)(2,1)S(1)} %get-tuple-element.21.vs, f32[128,2048]{1,0:T(8,128)S(1)} %get-tuple-element.22.own_s, ...), custom_call_target="tpu_custom_call" | custom-call | flops 201326592 | bytes 1048576 | tf_op jit(solution)/shard_map/rows/pallas_call | solution.py:523
  30.5 0.4 %collective-permute-done.15.got_ref = f32[264,128]{1,0:T(8,128)S(1)} collective-permute-done((f32[264,128]{1,0:T(8,128)S(1)}, f32[264,128]{1,0:T(8,128)S(1)}, u32[]{:S(2)}, u32[]{:S(2)}) %collective-permute-start.15) | collective-permute-done | bytes 135200 | tf_op jit(solution)/shard_map/ppermute | solution.py:567
  30.9 0.7 %join.1 = (f32[128,128]{1,0:T(8,128)}, f32[128,128]{1,0:T(8,128)}, f32[1,128]{1,0:T(1,128)}, bf16[128,128]{1,0:T(8,128)(2,1)}, f32[128,128]{1,0:T(8,128)}) custom-call(f32[264,128]{1,0:T(8,128)S(1)} %get-tuple-element.18.keep_ref, f32[264,128]{1,0:T(8,128)S(1)} %collective-permute-done.15.got_ref, bf16[128,128]{1,0:T(8,128)(2,1)S(1)} %get-tuple-element.24.rows_out, ...), custom_call_target="tpu_custom_call" | custom-call | tf_op jit(solution)/shard_map/join/pallas_call | solution.py:544
Async XLA Ops:
  1.5 8.1 %collective-permute-start = (bf16[528,128]{1,0:T(8,128)(2,1)S(1)}, bf16[528,128]{1,0:T(8,128)(2,1)S(1)}, u32[]{:S(2)}, u32[]{:S(2)}) collective-permute-start(bf16[528,128]{1,0:T(8,128)(2,1)S(1)} %pack.1.refs_0_.own), channel_id=1, source_target_pairs={{0,8},{1,9},{2,10},{3,11},{4,0},{5,1},{6,2},{7,3},{12,4},{13,5},{1... | collective-permute-start | bytes 405512 | tf_op jit(solution)/shard_map/ppermute | solution.py:567
  5.6 7.4 %collective-permute-start.3 = (bf16[528,128]{1,0:T(8,128)(2,1)S(1)}, bf16[528,128]{1,0:T(8,128)(2,1)S(1)}, u32[]{:S(2)}, u32[]{:S(2)}) collective-permute-start(bf16[528,128]{1,0:T(8,128)(2,1)S(1)} %pack.1.refs_0_.own), channel_id=1, source_target_pairs={{0,2},{1,3},{2,0},{3,1},{4,6},{5,7},{6,4},{7,5},{12,14},{13,15},{1... | collective-permute-start | bytes 405512 | tf_op jit(solution)/shard_map/ppermute | solution.py:567
  7.1 6.5 %collective-permute-start.1 = (bf16[528,128]{1,0:T(8,128)(2,1)S(1)}, bf16[528,128]{1,0:T(8,128)(2,1)S(1)}, u32[]{:S(2)}, u32[]{:S(2)}) collective-permute-start(bf16[528,128]{1,0:T(8,128)(2,1)S(1)} %pack.1.refs_0_.own), channel_id=1, source_target_pairs={{0,4},{1,5},{2,6},{3,7},{4,12},{5,13},{6,14},{7,15},{12,8},{13,9},... | collective-permute-start | bytes 405512 | tf_op jit(solution)/shard_map/ppermute | solution.py:567
  7.1 6.5 %collective-permute-start.2 = (bf16[528,128]{1,0:T(8,128)(2,1)S(1)}, bf16[528,128]{1,0:T(8,128)(2,1)S(1)}, u32[]{:S(2)}, u32[]{:S(2)}) collective-permute-start(bf16[528,128]{1,0:T(8,128)(2,1)S(1)} %pack.1.refs_0_.own), channel_id=1, source_target_pairs={{0,1},{1,0},{2,3},{3,2},{4,5},{5,4},{6,7},{7,6},{12,13},{13,12},{1... | collective-permute-start | bytes 405512 | tf_op jit(solution)/shard_map/ppermute | solution.py:567
  9.6 7.2 %collective-permute-start.4 = (bf16[528,128]{1,0:T(8,128)(2,1)S(1)}, bf16[528,128]{1,0:T(8,128)(2,1)S(1)}, u32[]{:S(2)}, u32[]{:S(2)}) collective-permute-start(bf16[528,128]{1,0:T(8,128)(2,1)S(1)} %collective-permute-done.refs_1_), channel_id=1, source_target_pairs={{0,8},{1,9},{2,10},{3,11},{4,0},{5,1},{6,2},{7,3},{12,4},{13,5},{1... | collective-permute-start | bytes 405512 | tf_op jit(solution)/shard_map/ppermute | solution.py:567
  13.0 5.3 %collective-permute-start.11 = (bf16[528,128]{1,0:T(8,128)(2,1)S(1)}, bf16[528,128]{1,0:T(8,128)(2,1)S(1)}, u32[]{:S(2)}, u32[]{:S(2)}) collective-permute-start(bf16[528,128]{1,0:T(8,128)(2,1)S(1)} %collective-permute-done.3.refs_4_), channel_id=1, source_target_pairs={{0,1},{1,0},{2,3},{3,2},{4,5},{5,4},{6,7},{7,6},{12,13},{13,12},{1... | collective-permute-start | bytes 405512 | tf_op jit(solution)/shard_map/ppermute | solution.py:567
  13.0 7.1 %collective-permute-start.6 = (bf16[528,128]{1,0:T(8,128)(2,1)S(1)}, bf16[528,128]{1,0:T(8,128)(2,1)S(1)}, u32[]{:S(2)}, u32[]{:S(2)}) collective-permute-start(bf16[528,128]{1,0:T(8,128)(2,1)S(1)} %collective-permute-done.3.refs_4_), channel_id=1, source_target_pairs={{0,4},{1,5},{2,6},{3,7},{4,12},{5,13},{6,14},{7,15},{12,8},{13,9},... | collective-permute-start | bytes 405512 | tf_op jit(solution)/shard_map/ppermute | solution.py:567
  13.7 6.4 %collective-permute-start.7 = (bf16[528,128]{1,0:T(8,128)(2,1)S(1)}, bf16[528,128]{1,0:T(8,128)(2,1)S(1)}, u32[]{:S(2)}, u32[]{:S(2)}) collective-permute-start(bf16[528,128]{1,0:T(8,128)(2,1)S(1)} %collective-permute-done.1.refs_2_), channel_id=1, source_target_pairs={{0,1},{1,0},{2,3},{3,2},{4,5},{5,4},{6,7},{7,6},{12,13},{13,12},{1... | collective-permute-start | bytes 405512 | tf_op jit(solution)/shard_map/ppermute | solution.py:567
  13.7 6.9 %collective-permute-start.5 = (bf16[528,128]{1,0:T(8,128)(2,1)S(1)}, bf16[528,128]{1,0:T(8,128)(2,1)S(1)}, u32[]{:S(2)}, u32[]{:S(2)}) collective-permute-start(bf16[528,128]{1,0:T(8,128)(2,1)S(1)} %collective-permute-done.refs_1_), channel_id=1, source_target_pairs={{0,2},{1,3},{2,0},{3,1},{4,6},{5,7},{6,4},{7,5},{12,14},{13,15},{1... | collective-permute-start | bytes 405512 | tf_op jit(solution)/shard_map/ppermute | solution.py:567
  16.8 5.8 %collective-permute-start.8 = (bf16[528,128]{1,0:T(8,128)(2,1)S(1)}, bf16[528,128]{1,0:T(8,128)(2,1)S(1)}, u32[]{:S(2)}, u32[]{:S(2)}) collective-permute-start(bf16[528,128]{1,0:T(8,128)(2,1)S(1)} %collective-permute-done.4.refs_5_), channel_id=1, source_target_pairs={{0,2},{1,3},{2,0},{3,1},{4,6},{5,7},{6,4},{7,5},{12,14},{13,15},{1... | collective-permute-start | bytes 405512 | tf_op jit(solution)/shard_map/ppermute | solution.py:567
  18.3 4.3 %collective-permute-start.9 = (bf16[528,128]{1,0:T(8,128)(2,1)S(1)}, bf16[528,128]{1,0:T(8,128)(2,1)S(1)}, u32[]{:S(2)}, u32[]{:S(2)}) collective-permute-start(bf16[528,128]{1,0:T(8,128)(2,1)S(1)} %collective-permute-done.refs_1_), channel_id=1, source_target_pairs={{0,1},{1,0},{2,3},{3,2},{4,5},{5,4},{6,7},{7,6},{12,13},{13,12},{1... | collective-permute-start | bytes 405512 | tf_op jit(solution)/shard_map/ppermute | solution.py:567
  20.1 2.5 %collective-permute-start.13 = (bf16[528,128]{1,0:T(8,128)(2,1)S(1)}, bf16[528,128]{1,0:T(8,128)(2,1)S(1)}, u32[]{:S(2)}, u32[]{:S(2)}) collective-permute-start(bf16[528,128]{1,0:T(8,128)(2,1)S(1)} %collective-permute-done.4.refs_5_), channel_id=1, source_target_pairs={{0,1},{1,0},{2,3},{3,2},{4,5},{5,4},{6,7},{7,6},{12,13},{13,12},{1... | collective-permute-start | bytes 405512 | tf_op jit(solution)/shard_map/ppermute | solution.py:567
  20.1 2.5 %collective-permute-start.12 = (bf16[528,128]{1,0:T(8,128)(2,1)S(1)}, bf16[528,128]{1,0:T(8,128)(2,1)S(1)}, u32[]{:S(2)}, u32[]{:S(2)}) collective-permute-start(bf16[528,128]{1,0:T(8,128)(2,1)S(1)} %collective-permute-done.6.refs_7_), channel_id=1, source_target_pairs={{0,1},{1,0},{2,3},{3,2},{4,5},{5,4},{6,7},{7,6},{12,13},{13,12},{1... | collective-permute-start | bytes 405512 | tf_op jit(solution)/shard_map/ppermute | solution.py:567
  20.6 2.0 %collective-permute-start.10 = (bf16[528,128]{1,0:T(8,128)(2,1)S(1)}, bf16[528,128]{1,0:T(8,128)(2,1)S(1)}, u32[]{:S(2)}, u32[]{:S(2)}) collective-permute-start(bf16[528,128]{1,0:T(8,128)(2,1)S(1)} %collective-permute-done.5.refs_6_), channel_id=1, source_target_pairs={{0,1},{1,0},{2,3},{3,2},{4,5},{5,4},{6,7},{7,6},{12,13},{13,12},{1... | collective-permute-start | bytes 405512 | tf_op jit(solution)/shard_map/ppermute | solution.py:567
  22.6 1.4 %collective-permute-start.14 = (bf16[528,128]{1,0:T(8,128)(2,1)S(1)}, bf16[528,128]{1,0:T(8,128)(2,1)S(1)}, u32[]{:S(2)}, u32[]{:S(2)}) collective-permute-start(bf16[528,128]{1,0:T(8,128)(2,1)S(1)} %collective-permute-done.8.refs_9_), channel_id=1, source_target_pairs={{0,1},{1,0},{2,3},{3,2},{4,5},{5,4},{6,7},{7,6},{12,13},{13,12},{1... | collective-permute-start | bytes 405512 | tf_op jit(solution)/shard_map/ppermute | solution.py:567
  29.5 1.4 %collective-permute-start.15 = (f32[264,128]{1,0:T(8,128)S(1)}, f32[264,128]{1,0:T(8,128)S(1)}, u32[]{:S(2)}, u32[]{:S(2)}) collective-permute-start(f32[264,128]{1,0:T(8,128)S(1)} %get-tuple-element.19), channel_id=1, source_target_pairs={{0,1},{1,0},{2,3},{3,2},{4,5},{5,4},{6,7},{7,6},{12,13},{13,12},{1... | collective-permute-start | bytes 405512 | tf_op jit(solution)/shard_map/ppermute | solution.py:567
